TPU v7x, 32 devices: a whole 2x2x4 slice. The times are simulated.
32 devices in a mesh: ctx: 16 (over z, y, x), head: 2 (over core).
Axes of the slice: x: 2, y: 2, z: 4, core: 2. Of those that a mesh axis runs over, the one named last changes fastest.
Arguments:
- q_home: bfloat16 [8192, 2048], P('ctx', 'head'), may hold values from -18 to 18
- k_home: bfloat16 [8192, 512], P('ctx', 'head'), may hold values from -6 to 6
- value_slots_local: bfloat16 [8192, 512], P('ctx', 'head'), may hold values from -16 to 16
- out_weight: bfloat16 [2048, 4096], P('head'), may hold values from -0.125 to 0.125
- router: float32 [8192], P('ctx'), may hold values from 0.25 to 1
- positions: int32 [8192], P('ctx'), may hold values from 0 to 32767, as said below
- counts: int32 [16], P('ctx'), may hold values from 1 to 512, 2048 in all
Outputs:
- routed_update: bfloat16 [8192, 4096], P('ctx', 'head')
Inputs may be any that keep to these rules, and one draw needn't show every extreme that they name: counts sum to 2048; the busiest shard holds exactly 512. The 512 positions of shard d are distinct, increasing, and lie in [d * 2048, (d + 1) * 2048).
All inputs are finite; a program needn't handle non-finite values.
Results may differ from a plain program's by a relative error of at most 0.033.
Values may be sent and summed in bfloat16 or wider, within the bound.
A program may use at most 128 MiB of HBM per device.

v0:
```python
import functools

import jax
import jax.numpy as jnp
from jax import lax
from jax.experimental import pallas as pl
from jax.experimental.pallas import tpu as pltpu
from jax.sharding import PartitionSpec as P

HEAD_WIDTH = 128
PICKED_PER_SHARD = 128
QUERY_BLOCK = 128
TILE = 16
SWAP_PARTS = 4
LANES = 128
FAR = 1 << 28
LOW = -1e30

rope_theta = 500000.0


def inverse_freqs():
    half_dim = HEAD_WIDTH // 2
    return rope_theta ** (-(jnp.arange(half_dim, dtype=jnp.float32) * 2.0 / HEAD_WIDTH))


def angle_tables(positions):
    angles = positions.astype(jnp.float32)[:, None] * inverse_freqs()[None, :]
    cosine, sine = jnp.cos(angles), jnp.sin(angles)
    return (
        jnp.concatenate([cosine, cosine], axis=1),
        jnp.concatenate([-sine, sine], axis=1),
    )


def rotate(rows, cosine, sine):
    heads = rows.shape[1] // HEAD_WIDTH
    x = rows.astype(jnp.float32).reshape(rows.shape[0], heads, HEAD_WIDTH)
    swapped = jnp.roll(x, HEAD_WIDTH // 2, axis=2)
    turned = x * cosine[:, None, :] + swapped * sine[:, None, :]
    return turned.reshape(rows.shape).astype(jnp.bfloat16)


def prefix_rows(x):
    rows = x.shape[0]
    row = lax.broadcasted_iota(jnp.int32, x.shape, 0)
    total = jnp.zeros_like(x)
    for e in range(rows - 1):
        total += jnp.where(row > e, x[e : e + 1, :], 0)
    return total


def spread_kernel(
    shards,
    kv_ref,
    cnt_ref,
    weight_ref,
    all_ref,
    cnt_all,
    swap_ref,
    recv,
    packed,
    send_sem,
    recv_sem,
    own_sem,
    swap_sem,
):
    me = lax.axis_index("ctx")
    other = 1 - lax.axis_index("head")
    rows = kv_ref.shape[1]
    slots = shards * rows
    width = kv_ref.shape[2]
    pieces = packed.shape[0]
    shift = shards.bit_length() - 1
    peers = [lax.rem(me + o, shards) for o in range(shards)]

    barrier = pltpu.get_barrier_semaphore()
    for o in range(1, shards):
        pl.semaphore_signal(barrier, inc=1, device_id={"ctx": peers[o]})
    pl.semaphore_signal(barrier, inc=1, device_id={"head": other})
    own_kv = pltpu.make_async_copy(kv_ref.at[0], recv.at[me], own_sem.at[0])
    own_kv.start()
    own_cnt = pltpu.make_async_copy(cnt_ref, cnt_all.at[me], own_sem.at[1])
    own_cnt.start()
    pl.semaphore_wait(barrier, shards)

    def remote(kind, o, src, dst):
        return pltpu.make_async_remote_copy(
            src_ref=src,
            dst_ref=dst,
            send_sem=send_sem.at[kind, o],
            recv_sem=recv_sem.at[kind, o],
            device_id={"ctx": peers[o]},
        )

    cnt_copies = [remote(0, o, cnt_ref, cnt_all.at[me]) for o in range(1, shards)]
    kv_copies = [remote(1, o, kv_ref.at[o], recv.at[me]) for o in range(1, shards)]
    for c in cnt_copies:
        c.start()
    for c in kv_copies:
        c.start()
    depth = weight_ref.shape[0] // SWAP_PARTS
    half = swap_ref.shape[1]
    columns = pl.ds(pl.multiple_of(other * half, half), half)
    swaps = []
    for i in range(SWAP_PARTS):
        at = pl.ds(i * depth, depth)
        swaps.append(
            pltpu.make_async_remote_copy(
                src_ref=weight_ref.at[at, columns],
                dst_ref=swap_ref.at[at, :],
                send_sem=swap_sem.at[0, i],
                recv_sem=swap_sem.at[1, i],
                device_id={"head": other},
            )
        )
    for c in swaps:
        c.start()
    own_kv.wait()
    own_cnt.wait()
    for c in cnt_copies:
        c.wait()
    counts = cnt_all[:, 0, :]
    source = lax.broadcasted_iota(jnp.int32, counts.shape, 0)
    lead = (me - source + shards) & (shards - 1)
    taken = (counts + (shards - 1) - lead) >> shift
    start = prefix_rows(taken)
    wide = (shards, slots)
    taken_w = jnp.broadcast_to(taken[:, :1], wide)
    start_w = jnp.broadcast_to(start[:, :1], wide)
    within = lax.broadcasted_iota(jnp.int32, wide, 1) - rows * lax.broadcasted_iota(
        jnp.int32, wide, 0
    )
    live = (within >= 0) & (within < taken_w)
    target = jnp.sum(jnp.where(live, start_w + within + 1, 0), axis=0, keepdims=True) - 1
    place = lax.broadcasted_iota(jnp.int32, (pieces * TILE, slots), 0)
    pick = jnp.where(place == target, 1.0, 0.0).astype(jnp.bfloat16)
    for c in kv_copies:
        c.wait()
    got = recv[...].reshape(slots, width)
    packed[...] = (
        jnp.dot(pick, got, preferred_element_type=jnp.float32)
        .astype(jnp.bfloat16)
        .reshape(packed.shape)
    )
    own_piece = pltpu.make_async_copy(packed, all_ref.at[:, me], own_sem.at[0])
    out_copies = [remote(2, o, packed, all_ref.at[:, me]) for o in range(1, shards)]
    for c in out_copies:
        c.start()
    own_piece.start()
    own_piece.wait()
    for c in out_copies:
        c.wait()
    for c in swaps:
        c.wait()


def spread(kv_send, counts, weight, shards, pieces):
    rows, width = kv_send.shape[1:]
    return pl.pallas_call(
        functools.partial(spread_kernel, shards),
        out_shape=(
            jax.ShapeDtypeStruct((pieces, shards, TILE, width), jnp.bfloat16),
            jax.ShapeDtypeStruct((shards, 8, LANES), jnp.int32),
            jax.ShapeDtypeStruct((weight.shape[0], weight.shape[1] // 2), weight.dtype),
        ),
        in_specs=[pl.BlockSpec(memory_space=pltpu.VMEM)] * 2
        + [pl.BlockSpec(memory_space=pl.ANY)],
        out_specs=(
            pl.BlockSpec(memory_space=pl.ANY),
            pl.BlockSpec(memory_space=pltpu.VMEM),
            pl.BlockSpec(memory_space=pl.ANY),
        ),
        scratch_shapes=[
            pltpu.VMEM((shards, rows, width), jnp.bfloat16),
            pltpu.VMEM((pieces, TILE, width), jnp.bfloat16),
            pltpu.SemaphoreType.DMA((3, shards)),
            pltpu.SemaphoreType.DMA((3, shards)),
            pltpu.SemaphoreType.DMA((2,)),
            pltpu.SemaphoreType.DMA((2, SWAP_PARTS)),
        ],
        compiler_params=pltpu.CompilerParams(collective_id=0, has_side_effects=True),
        name="spread",
    )(kv_send, counts, weight)


def attend_kernel(
    shards, q_ref, cos_ref, sin_ref, cnt_ref, kv_ref, out_ref, q_s, top_s, sum_s, acc_s
):
    me = lax.axis_index("ctx")
    step = pl.program_id(0)
    blocks, groups, stack, _ = q_s.shape
    share = stack // QUERY_BLOCK
    keys = kv_ref.shape[0]
    shift = shards.bit_length() - 1
    factor = 1.4426950408889634 / HEAD_WIDTH**0.5

    counts = cnt_ref[:, 0, :]
    shard_row = lax.broadcasted_iota(jnp.int32, counts.shape, 0)
    own_start = jnp.sum(jnp.where(shard_row < me, counts, 0)[:, :1])
    own_count = jnp.sum(jnp.where(shard_row == me, counts, 0)[:, :1])
    live_blocks = (own_count + (QUERY_BLOCK - 1)) >> (QUERY_BLOCK.bit_length() - 1)

    diagonal = shard_row == lax.broadcasted_iota(jnp.int32, counts.shape, 1)
    count_row = jnp.sum(jnp.where(diagonal, counts, 0), axis=0, keepdims=True)
    offset_row = jnp.sum(
        jnp.where(shard_row < lax.broadcasted_iota(jnp.int32, counts.shape, 1), counts, 0),
        axis=0,
        keepdims=True,
    )
    grid_shape = (keys, LANES)
    key_row = lax.broadcasted_iota(jnp.int32, grid_shape, 0)
    source = lax.broadcasted_iota(jnp.int32, grid_shape, 1)
    lead = ((key_row >> 4) - source) & (shards - 1)
    taken = jnp.where(source < shards, (count_row + (shards - 1) - lead) >> shift, 0)
    earlier = (
        lax.broadcasted_iota(jnp.int32, (LANES, LANES), 0)
        < lax.broadcasted_iota(jnp.int32, (LANES, LANES), 1)
    )
    start = jnp.dot(
        taken.astype(jnp.float32).astype(jnp.bfloat16),
        jnp.where(earlier, 1.0, 0.0).astype(jnp.bfloat16),
        preferred_element_type=jnp.float32,
    ).astype(jnp.int32)
    within = step * TILE + (key_row & (TILE - 1)) - start
    held = (within >= 0) & (within < taken)
    names = jnp.min(
        jnp.where(held, offset_row + within * shards + lead, FAR), axis=1, keepdims=True
    )
    first_name = jnp.min(names)

    @pl.when(step == 0)
    def _():
        top_s[...] = jnp.full_like(top_s, LOW)
        sum_s[...] = jnp.zeros_like(sum_s)
        acc_s[...] = jnp.zeros_like(acc_s)

        @pl.loop(0, live_blocks)
        def _(b):
            at = pl.ds(pl.multiple_of(b * QUERY_BLOCK, QUERY_BLOCK), QUERY_BLOCK)
            cosine, sine = cos_ref[at, :], sin_ref[at, :]
            for g in range(groups):
                for h in range(share):
                    cols = pl.ds((g * share + h) * HEAD_WIDTH, HEAD_WIDTH)
                    x = q_ref[at, cols].astype(jnp.float32)
                    turned = x * cosine + pltpu.roll(x, HEAD_WIDTH // 2, 1) * sine
                    q_s[b, g, pl.ds(h * QUERY_BLOCK, QUERY_BLOCK), :] = turned.astype(jnp.bfloat16)

    @pl.loop(0, live_blocks)
    def _(b):
        first_query = own_start + b * QUERY_BLOCK

        @pl.when(first_name < first_query + QUERY_BLOCK)
        def _():
            query = first_query + lax.broadcasted_iota(jnp.int32, (keys, QUERY_BLOCK), 1)
            bias = jnp.where(names <= query, 0.0, LOW)
            bias = jnp.concatenate([bias] * share, axis=1)
            for g in range(groups):
                key = kv_ref[:, pl.ds(g * HEAD_WIDTH, HEAD_WIDTH)]
                value = kv_ref[:, pl.ds((groups + g) * HEAD_WIDTH, HEAD_WIDTH)]
                scores = lax.dot_general(
                    key, q_s[b, g], (((1,), (1,)), ((), ())), preferred_element_type=jnp.float32
                )
                scores = scores * factor + bias
                old = top_s[b, g]
                top = jnp.maximum(old, jnp.max(scores, axis=0, keepdims=True))
                terms = jnp.exp2(scores - top)
                rescale = jnp.exp2(old - top)
                top_s[b, g] = top
                sum_s[b, g] = sum_s[b, g] * rescale + jnp.sum(terms, axis=0, keepdims=True)
                acc_s[b, g] = acc_s[b, g] * rescale + lax.dot_general(
                    value,
                    terms.astype(jnp.bfloat16),
                    (((0,), (0,)), ((), ())),
                    preferred_element_type=jnp.float32,
                )

    @pl.when(step == pl.num_programs(0) - 1)
    def _():
        for b in range(blocks):
            at = pl.ds(b * QUERY_BLOCK, QUERY_BLOCK)

            @pl.when(b < live_blocks)
            def _():
                for g in range(groups):
                    done = acc_s[b, g] / sum_s[b, g]
                    for h in range(share):
                        part = done[:, h * QUERY_BLOCK : (h + 1) * QUERY_BLOCK]
                        out_ref[at, pl.ds((g * share + h) * HEAD_WIDTH, HEAD_WIDTH)] = (
                            part.T.astype(jnp.bfloat16)
                        )

            @pl.when(b >= live_blocks)
            def _():
                out_ref[at, :] = jnp.zeros((QUERY_BLOCK, out_ref.shape[1]), jnp.bfloat16)


def attend(q_home, cosine, sine, cnt_all, kv_all, shards):
    slots, features = q_home.shape
    pieces, keys, width = kv_all.shape
    groups = width // (2 * HEAD_WIDTH)
    share = features // HEAD_WIDTH // groups
    blocks = slots // QUERY_BLOCK
    stack = share * QUERY_BLOCK
    whole = lambda a: pl.BlockSpec(a.shape, lambda i: (0,) * a.ndim)
    return pl.pallas_call(
        functools.partial(attend_kernel, shards),
        out_shape=jax.ShapeDtypeStruct((slots, features), jnp.bfloat16),
        grid=(pieces,),
        in_specs=[
            whole(q_home),
            whole(cosine),
            whole(sine),
            whole(cnt_all),
            pl.BlockSpec((None, keys, width), lambda i: (i, 0, 0)),
        ],
        out_specs=pl.BlockSpec((slots, features), lambda i: (0, 0)),
        scratch_shapes=[
            pltpu.VMEM((blocks, groups, stack, HEAD_WIDTH), jnp.bfloat16),
            pltpu.VMEM((blocks, groups, 1, stack), jnp.float32),
            pltpu.VMEM((blocks, groups, 1, stack), jnp.float32),
            pltpu.VMEM((blocks, groups, HEAD_WIDTH, stack), jnp.float32),
        ],
        name="attend",
    )(q_home, cosine, sine, cnt_all, kv_all)


def trade_kernel(mine_ref, theirs_ref, sems):
    other = 1 - lax.axis_index("head")
    barrier = pltpu.get_barrier_semaphore()
    pl.semaphore_signal(barrier, inc=1, device_id={"head": other})
    pl.semaphore_wait(barrier, 1)
    depth = mine_ref.shape[0] // SWAP_PARTS
    copies = []
    for i in range(SWAP_PARTS):
        at = pl.ds(i * depth, depth)
        copies.append(
            pltpu.make_async_remote_copy(
                src_ref=mine_ref.at[at, :],
                dst_ref=theirs_ref.at[at, :],
                send_sem=sems.at[0, i],
                recv_sem=sems.at[1, i],
                device_id={"head": other},
            )
        )
    for c in copies:
        c.start()
    for c in copies:
        c.wait()


def trade(mine):
    return pl.pallas_call(
        trade_kernel,
        out_shape=jax.ShapeDtypeStruct(mine.shape, mine.dtype),
        in_specs=[pl.BlockSpec(memory_space=pl.ANY)],
        out_specs=pl.BlockSpec(memory_space=pl.ANY),
        scratch_shapes=[pltpu.SemaphoreType.DMA((2, SWAP_PARTS))],
        compiler_params=pltpu.CompilerParams(collective_id=1, has_side_effects=True),
        name="trade",
    )(mine)


def project_kernel(head_ref, count_ref, mine_ref, theirs_ref, own_w, got_w, router_ref, out_ref):
    blocks = mine_ref.shape[0] // QUERY_BLOCK
    count = count_ref[0]
    square = (QUERY_BLOCK, QUERY_BLOCK)
    row = lax.broadcasted_iota(jnp.int32, square, 0)
    diagonal = row == lax.broadcasted_iota(jnp.int32, square, 1)
    for b in range(blocks):
        at = pl.ds(b * QUERY_BLOCK, QUERY_BLOCK)

        @pl.when(b * QUERY_BLOCK < count)
        def _():
            summed = jnp.dot(mine_ref[at, :], own_w[...], preferred_element_type=jnp.float32)
            summed += jnp.dot(theirs_ref[at, :], got_w[...], preferred_element_type=jnp.float32)
            summed = summed.astype(jnp.bfloat16).astype(jnp.float32)
            gain = jnp.sum(
                jnp.where(diagonal, router_ref[b : b + 1, :], 0.0), axis=1, keepdims=True
            )
            live = b * QUERY_BLOCK + row[:, :1] < count
            out_ref[at, :] = jnp.where(live, gain * summed, 0.0).astype(jnp.bfloat16)

        @pl.when(b * QUERY_BLOCK >= count)
        def _():
            out_ref[at, :] = jnp.zeros((QUERY_BLOCK, out_ref.shape[1]), jnp.bfloat16)


def project(head, counts, mine, theirs, weight, swapped, router):
    slots, features = mine.shape
    half = swapped.shape[1]
    tile = min(512, half)
    tiles = half // tile
    gains = router.reshape(slots // QUERY_BLOCK, QUERY_BLOCK)
    whole = lambda a: pl.BlockSpec(a.shape, lambda i, h, c: (0,) * a.ndim)
    return pl.pallas_call(
        project_kernel,
        out_shape=jax.ShapeDtypeStruct((slots, half), jnp.bfloat16),
        grid_spec=pltpu.PrefetchScalarGridSpec(
            num_scalar_prefetch=2,
            grid=(tiles,),
            in_specs=[
                whole(mine),
                whole(theirs),
                pl.BlockSpec((features, tile), lambda i, h, c: (0, h[0] * tiles + i)),
                pl.BlockSpec((features, tile), lambda i, h, c: (0, i)),
                whole(gains),
            ],
            out_specs=pl.BlockSpec((slots, tile), lambda i, h, c: (0, i)),
        ),
        name="project",
    )(head, counts, mine, theirs, weight, swapped, gains)


def local(q_home, k_home, value_slots_local, out_weight, router, positions, counts):
    shards = lax.axis_size("ctx")
    slot_count = q_home.shape[0]
    peer_rows = slot_count // shards
    cap = PICKED_PER_SHARD + (shards - 1) // 2
    pieces = -(-cap // TILE)
    cosine, sine = angle_tables(positions)
    kv = jnp.concatenate([rotate(k_home, cosine, sine), value_slots_local], axis=1)
    width = kv.shape[1]
    kv_send = kv.reshape(peer_rows, shards, width).transpose(1, 0, 2)
    short = max(0, TILE - peer_rows)
    kv_send = jnp.pad(kv_send, ((0, 0), (0, short), (0, 0)))
    own = jnp.broadcast_to(counts[:, None], (8, LANES))
    kv_all, cnt_all, swapped = spread(kv_send, own, out_weight, shards, pieces)
    kv_all = kv_all.reshape(pieces, shards * TILE, width)
    attended = attend(q_home, cosine, sine, cnt_all, kv_all, shards)
    theirs = trade(attended)
    head = lax.axis_index("head").astype(jnp.int32).reshape(1)
    return project(head, counts, attended, theirs, out_weight, swapped, router)


def solution(mesh):
    return jax.shard_map(
        local,
        mesh=mesh,
        in_specs=(
            P("ctx", "head"),
            P("ctx", "head"),
            P("ctx", "head"),
            P("head", None),
            P("ctx"),
            P("ctx"),
            P("ctx"),
        ),
        out_specs=P("ctx", "head"),
        check_vma=False,
    )
```

profile of v0, /device:TPU:29, one launch (start us, length us, event | category | flops | bytes accessed | tf_op | source)
XLA Modules:
  0.0 138.2 jit_solution(9374907855645788445)
XLA Ops:
  0.0 0.0 copy-start.2
  0.7 0.7 convert_element_type.9
  1.4 0.6 broadcast_in_dim.5.cnt_ref
  2.0 1.2 reshape.31
  3.2 0.0 copy-start.3
  3.2 0.6 fusion.2
  3.8 1.0 fusion.1
  4.8 0.2 pad_maximum_fusion.1
  5.0 0.0 copy-start
  5.0 0.0 copy-start.1
  5.0 0.6 maximum_multiply_fusion
  5.7 0.2 mul.42
  5.9 0.0 copy-done.2
  5.9 0.1 fusion
  6.0 0.0 copy-done.3
  6.1 1.1 copy.14
  7.2 85.0 %spread.1 = (bf16[9,16,16,512]{3,2,1,0:T(8,128)(2,1)}, s32[16,8,128]{2,1,0:T(8,128)}, bf16[1024,2048]{1,0:T(8,128)(2,1)}) custom-call(bf16[16,32,512]{2,1,0:T(8,128)(2,1)} %bitcast.21, s32[8,128]{1,0:T(8,128)} %broadcast_in_dim.5.cnt_ref, bf16[1024,4096]{1,0:T(8,128)(2,1)} %own_w.1), custom_call_target="tpu_custom_call" | custom-call | tf_op jit(solution)/shard_map/spread/pallas_call | solution.py:160
  92.2 0.0 copy-done
  92.2 0.0 copy-done.1
  92.2 32.2 %attend.1.mine_ref = bf16[512,1024]{1,0:T(8,128)(2,1)} custom-call(bf16[512,1024]{1,0:T(8,128)(2,1)} %q_ref.1, f32[512,128]{1,0:T(8,128)} %copy-done, f32[512,128]{1,0:T(8,128)} %copy-done.1, s32[16,8,128]{2,1,0:T(8,128)} %get-tuple-element.8.cnt_ref, bf16[9,256,512]{2,1,0:T(8,128)(2,1)} %bitcast.19), custom_call_target="tpu_custom_call" | custom-call | tf_op jit(solution)/shard_map/attend/pallas_call | solution.py:306
  124.4 3.3 %trade.1.theirs_ref = bf16[512,1024]{1,0:T(8,128)(2,1)} custom-call(bf16[512,1024]{1,0:T(8,128)(2,1)} %attend.1.mine_ref), custom_call_target="tpu_custom_call" | custom-call | tf_op jit(solution)/shard_map/trade/pallas_call | solution.py:353
  127.7 10.5 %project.1 = bf16[512,2048]{1,0:T(8,128)(2,1)} custom-call(s32[1]{0:T(128)} %bitcast.head_ref, s32[1]{0:T(128)} %copy.15.count_ref, bf16[512,1024]{1,0:T(8,128)(2,1)} %attend.1.mine_ref, bf16[512,1024]{1,0:T(8,128)(2,1)} %trade.1.theirs_ref, bf16[1024,4096]{1,0:T(8,128)(2,1)} %own_w.1, bf16[1024,2048]{1,0:T(8,128)(2,1)} %get-tuple-element.10.got_w, ...), custom_call_target="tpu_custom_call" | custom-call | tf_op jit(solution)/shard_map/project/pallas_call | solution.py:396
  (2 shorter events, 0.0 us)
Async XLA Ops:
  0.0 5.9 %copy-start.2 = (bf16[512,256]{1,0:T(8,128)(2,1)S(1)}, bf16[512,256]{1,0:T(8,128)(2,1)}, u32[]{:S(2)}) copy-start(bf16[512,256]{1,0:T(8,128)(2,1)} %param.8) | copy-start | bytes 786436
  3.2 2.8 %copy-start.3 = (bf16[512,256]{1,0:T(8,128)(2,1)S(1)}, bf16[512,256]{1,0:T(8,128)(2,1)}, u32[]{:S(2)}) copy-start(bf16[512,256]{1,0:T(8,128)(2,1)} %param.9) | copy-start | bytes 786436
  5.0 87.2 %copy-start = (f32[512,128]{1,0:T(8,128)}, f32[512,128]{1,0:T(8,128)S(1)}, u32[]{:S(2)}) copy-start(f32[512,128]{1,0:T(8,128)S(1)} %get-tuple-element.16.cos_ref) | copy-start | bytes 786436
  5.0 87.2 %copy-start.1 = (f32[512,128]{1,0:T(8,128)}, f32[512,128]{1,0:T(8,128)S(1)}, u32[]{:S(2)}) copy-start(f32[512,128]{1,0:T(8,128)S(1)} %get-tuple-element.17.sin_ref) | copy-start | bytes 786436
where the time goes:
time: 137 us; the launch traced here: 138 us
  Pallas kernels  131 us (96%)
  local copies, waits for them, and re-layouts  3.69 us (3%)
  other arithmetic  2.71 us (2%)
    pallas_call x1, Pallas kernels, spread(): pl.pallas_call(functools.partial(spread_kernel, shards), out_shape=(jax.S...  85 us
    pallas_call x1, Pallas kernels, attend(): pl.pallas_call(functools.partial(attend_kernel, shards), out_shape=jax.Sh...  32.2 us
    pallas_call x1, Pallas kernels, project(): pl.pallas_call(project_kernel, out_shape=jax.ShapeDtypeStruct((slots, hal...  10.5 us
    pallas_call x1, Pallas kernels, trade(): pl.pallas_call(trade_kernel, out_shape=jax.ShapeDtypeStruct(mine.shape, m...  3.34 us

commit v1 on v0

--- a/solution.py
+++ b/solution.py
@@ -48,6 +48,159 @@
     for e in range(rows - 1):
         total += jnp.where(row > e, x[e : e + 1, :], 0)
     return total
+
+
+def arrange(shards):
+    side = 1 << ((shards.bit_length() - 1) // 3)
+    return shards // (side * side), side * side
+
+
+def gather(shards, packed, all_ref, line_sem, plane_sem, relay_sem):
+    lines, plane = arrange(shards)
+    me = lax.axis_index("ctx")
+    z, spot = me // plane, me % plane
+    square = plane == 4
+    direct = (1, 2) if square else tuple(range(1, plane))
+    pieces = packed.shape[0]
+    cut = pieces // 2
+    halves = (pl.ds(0, cut), pl.ds(cut, pieces - cut))
+    labels = [(0, 0)] + [(way, t) for t in range(1, lines) for way in (1, -1)]
+
+    def valid(way, t):
+        if way == 0:
+            return True
+        return z - t >= 0 if way == 1 else z + t < lines
+
+    def when(way, t, body):
+        if way == 0:
+            body()
+        else:
+            pl.when(valid(way, t))(body)
+
+    def line_of(way, t):
+        return z - way * t
+
+    def source(label):
+        way, t = labels[label]
+        return packed if label == 0 else all_ref.at[:, line_of(way, t) * plane + spot]
+
+    def hop(label, way):
+        own_way, t = labels[label]
+        arriving = labels.index((way, t + 1))
+        target = line_of(own_way, t) * plane + spot
+        return pltpu.make_async_remote_copy(
+            src_ref=source(label),
+            dst_ref=all_ref.at[:, target],
+            send_sem=line_sem.at[0, arriving],
+            recv_sem=line_sem.at[1, arriving],
+            device_id={"ctx": me + way * plane},
+        )
+
+    def hop_in(label):
+        way, t = labels[label]
+        here = all_ref.at[:, line_of(way, t) * plane + spot]
+        return pltpu.make_async_remote_copy(
+            src_ref=here,
+            dst_ref=here,
+            send_sem=line_sem.at[0, label],
+            recv_sem=line_sem.at[1, label],
+            device_id={"ctx": me - way * plane},
+        )
+
+    def across(label, o):
+        way, t = labels[label]
+        return pltpu.make_async_remote_copy(
+            src_ref=source(label),
+            dst_ref=all_ref.at[:, line_of(way, t) * plane + spot],
+            send_sem=plane_sem.at[0, label, o],
+            recv_sem=plane_sem.at[1, label, o],
+            device_id={"ctx": z * plane + (spot ^ o)},
+        )
+
+    def across_in(label, o):
+        way, t = labels[label]
+        here = all_ref.at[:, line_of(way, t) * plane + (spot ^ o)]
+        return pltpu.make_async_remote_copy(
+            src_ref=here,
+            dst_ref=here,
+            send_sem=plane_sem.at[0, label, o],
+            recv_sem=plane_sem.at[1, label, o],
+            device_id={"ctx": z * plane + (spot ^ o)},
+        )
+
+    def relay(label, part, peer):
+        way, t = labels[label]
+        here = all_ref.at[halves[part], line_of(way, t) * plane + (spot ^ peer)]
+        return pltpu.make_async_remote_copy(
+            src_ref=here,
+            dst_ref=here,
+            send_sem=relay_sem.at[0, label, part],
+            recv_sem=relay_sem.at[1, label, part],
+            device_id={"ctx": z * plane + (spot ^ (3 - peer))},
+        )
+
+    def relay_in(label, part):
+        way, t = labels[label]
+        here = all_ref.at[halves[part], line_of(way, t) * plane + (spot ^ 3)]
+        return pltpu.make_async_remote_copy(
+            src_ref=here,
+            dst_ref=here,
+            send_sem=relay_sem.at[0, label, part],
+            recv_sem=relay_sem.at[1, label, part],
+            device_id={"ctx": z * plane + (spot ^ 3)},
+        )
+
+    def onward(label):
+        way, t = labels[label]
+        for next_way in (1, -1) if way == 0 else (way,):
+            if t + 1 < lines:
+                edge = z + 1 < lines if next_way == 1 else z - 1 >= 0
+                yield next_way, edge
+
+    def pass_on(label):
+        for next_way, edge in onward(label):
+            pl.when(edge)(hop(label, next_way).start)
+        for o in direct:
+            across(label, o).start()
+
+    def relay_label(label):
+        for part, peer in ((0, 1), (1, 2)):
+            across_in(label, peer).wait_recv()
+            if square:
+                relay(label, part, peer).start()
+
+    def relay_far(label):
+        for o in direct:
+            across_in(label, o).wait_recv()
+
+    def finish(label):
+        if square:
+            for part, peer in ((0, 1), (1, 2)):
+                relay_in(label, part).wait_recv()
+                relay(label, part, peer).wait_send()
+        for next_way, edge in onward(label):
+            pl.when(edge)(hop(label, next_way).wait_send)
+        for o in direct:
+            across(label, o).wait_send()
+
+    def arrive(label):
+        hop_in(label).wait_recv()
+        pass_on(label)
+
+    take = relay_label if square else relay_far
+    pass_on(0)
+    for t in range(1, lines):
+        for label, (way, steps) in enumerate(labels):
+            if steps == t:
+                when(way, steps, functools.partial(arrive, label))
+        for label, (way, steps) in enumerate(labels):
+            if steps == t - 1:
+                when(way, steps, functools.partial(take, label))
+    for label, (way, steps) in enumerate(labels):
+        if steps == lines - 1:
+            when(way, steps, functools.partial(take, label))
+    for label, (way, steps) in enumerate(labels):
+        when(way, steps, functools.partial(finish, label))
 
 
 def spread_kernel(
@@ -64,6 +217,9 @@
     recv_sem,
     own_sem,
     swap_sem,
+    line_sem,
+    plane_sem,
+    relay_sem,
 ):
     me = lax.axis_index("ctx")
     other = 1 - lax.axis_index("head")
@@ -144,19 +300,16 @@
         .reshape(packed.shape)
     )
     own_piece = pltpu.make_async_copy(packed, all_ref.at[:, me], own_sem.at[0])
-    out_copies = [remote(2, o, packed, all_ref.at[:, me]) for o in range(1, shards)]
-    for c in out_copies:
-        c.start()
     own_piece.start()
+    gather(shards, packed, all_ref, line_sem, plane_sem, relay_sem)
     own_piece.wait()
-    for c in out_copies:
-        c.wait()
     for c in swaps:
         c.wait()
 
 
 def spread(kv_send, counts, weight, shards, pieces):
     rows, width = kv_send.shape[1:]
+    lines, plane = arrange(shards)
     return pl.pallas_call(
         functools.partial(spread_kernel, shards),
         out_shape=(
@@ -174,10 +327,13 @@
         scratch_shapes=[
             pltpu.VMEM((shards, rows, width), jnp.bfloat16),
             pltpu.VMEM((pieces, TILE, width), jnp.bfloat16),
-            pltpu.SemaphoreType.DMA((3, shards)),
-            pltpu.SemaphoreType.DMA((3, shards)),
+            pltpu.SemaphoreType.DMA((2, shards)),
+            pltpu.SemaphoreType.DMA((2, shards)),
             pltpu.SemaphoreType.DMA((2,)),
             pltpu.SemaphoreType.DMA((2, SWAP_PARTS)),
+            pltpu.SemaphoreType.DMA((2, 2 * lines - 1)),
+            pltpu.SemaphoreType.DMA((2, 2 * lines - 1, plane)),
+            pltpu.SemaphoreType.DMA((2, 2 * lines - 1, 2)),
         ],
         compiler_params=pltpu.CompilerParams(collective_id=0, has_side_effects=True),
         name="spread",

time: 137 us -> 99.1 us (0.72); the launches traced: 138 us -> 97.9 us
  Pallas kernels: 131 us -> 90.7 us
    pallas_call x1, Pallas kernels: 85 us -> 42.7 us  [spread(): pl.pallas_call(functools.partial(spread_kernel, shards), out_shape=(jax.S...]
    pallas_call x1, Pallas kernels: 3.34 us -> 5.33 us  [trade(): pl.pallas_call(trade_kernel, out_shape=jax.ShapeDtypeStruct(mine.shape, m...]
where the time goes in v1:
time: 99.1 us; the launch traced here: 97.9 us
  Pallas kernels  90.7 us (92%)
  local copies, waits for them, and re-layouts  3.69 us (4%)
  other arithmetic  2.71 us (3%)
    pallas_call x1, Pallas kernels, spread(): pl.pallas_call(functools.partial(spread_kernel, shards), out_shape=(jax.S...  42.7 us
    pallas_call x1, Pallas kernels, attend(): pl.pallas_call(functools.partial(attend_kernel, shards), out_shape=jax.Sh...  32.2 us
    pallas_call x1, Pallas kernels, project(): pl.pallas_call(project_kernel, out_shape=jax.ShapeDtypeStruct((slots, hal...  10.5 us
    pallas_call x1, Pallas kernels, trade(): pl.pallas_call(trade_kernel, out_shape=jax.ShapeDtypeStruct(mine.shape, m...  5.33 us

profile of v1, /device:TPU:29, one launch (start us, length us, event | category | flops | bytes accessed | tf_op | source)
XLA Modules:
  0.0 97.9 jit_solution(13620656173758575449)
XLA Ops:
  0.0 0.0 copy-start.2
  0.7 0.7 convert_element_type.9
  1.4 0.6 broadcast_in_dim.5.cnt_ref
  2.0 1.2 %reshape.31 = f32[512,2,128]{2,1,0:T(2,128)S(1)} reshape(bf16[512,256]{1,0:T(8,128)(2,1)} %param.8) | data formatting | bytes 786432 | tf_op jit(solution)/shard_map/reshape | solution.py:38
  3.2 0.0 copy-start.3
  3.2 0.6 fusion.2
  3.8 1.0 %fusion.1 = (f32[512,64]{1,0:T(8,128)S(1)}, f32[512,64]{1,0:T(8,128)S(1)}, f32[512,64]{1,0:T(8,128)S(1)}) fusion(f32[64]{0:T(128)S(1)} %negate_power_fusion, f32[512]{0:T(512)S(1)} %convert_element_type.9), kind=kLoop, calls=%fused_computation.10 | loop fusion | flops 65536 | bytes 395520 | tf_op jit(solution)/shard_map/neg | solution.py:32
  4.8 0.2 pad_maximum_fusion.1
  5.0 0.0 copy-start
  5.0 0.0 copy-start.1
  5.0 0.6 maximum_multiply_fusion
  5.7 0.2 mul.42
  5.9 0.0 copy-done.2
  5.9 0.1 fusion
  6.0 0.0 copy-done.3
  6.1 1.1 %copy.14 = bf16[32,16,512]{2,0,1:T(8,128)(2,1)} copy(bf16[32,16,512]{2,1,0:T(8,128)(2,1)S(1)} %bitcast.23) | data formatting | bytes 1048576 | tf_op jit(solution)/shard_map/reshape | solution.py:580
  7.2 42.7 %spread.1 = (bf16[9,16,16,512]{3,2,1,0:T(8,128)(2,1)}, s32[16,8,128]{2,1,0:T(8,128)}, bf16[1024,2048]{1,0:T(8,128)(2,1)}) custom-call(bf16[16,32,512]{2,1,0:T(8,128)(2,1)} %bitcast.21, s32[8,128]{1,0:T(8,128)} %broadcast_in_dim.5.cnt_ref, bf16[1024,4096]{1,0:T(8,128)(2,1)} %own_w.1), custom_call_target="tpu_custom_call" | custom-call | tf_op jit(solution)/shard_map/spread/pallas_call | solution.py:313
  49.9 0.0 copy-done
  49.9 0.0 copy-done.1
  49.9 32.2 %attend.1.mine_ref = bf16[512,1024]{1,0:T(8,128)(2,1)} custom-call(bf16[512,1024]{1,0:T(8,128)(2,1)} %q_ref.1, f32[512,128]{1,0:T(8,128)} %copy-done, f32[512,128]{1,0:T(8,128)} %copy-done.1, s32[16,8,128]{2,1,0:T(8,128)} %get-tuple-element.8.cnt_ref, bf16[9,256,512]{2,1,0:T(8,128)(2,1)} %bitcast.19), custom_call_target="tpu_custom_call" | custom-call | tf_op jit(solution)/shard_map/attend/pallas_call | solution.py:462
  82.1 5.3 %trade.1.theirs_ref = bf16[512,1024]{1,0:T(8,128)(2,1)} custom-call(bf16[512,1024]{1,0:T(8,128)(2,1)} %attend.1.mine_ref), custom_call_target="tpu_custom_call" | custom-call | tf_op jit(solution)/shard_map/trade/pallas_call | solution.py:509
  87.4 10.5 %project.1 = bf16[512,2048]{1,0:T(8,128)(2,1)} custom-call(s32[1]{0:T(128)} %bitcast.head_ref, s32[1]{0:T(128)} %copy.15.count_ref, bf16[512,1024]{1,0:T(8,128)(2,1)} %attend.1.mine_ref, bf16[512,1024]{1,0:T(8,128)(2,1)} %trade.1.theirs_ref, bf16[1024,4096]{1,0:T(8,128)(2,1)} %own_w.1, bf16[1024,2048]{1,0:T(8,128)(2,1)} %get-tuple-element.10.got_w, ...), custom_call_target="tpu_custom_call" | custom-call | tf_op jit(solution)/shard_map/project/pallas_call | solution.py:552
  (2 shorter events, 0.0 us)
Async XLA Ops:
  0.0 5.9 %copy-start.2 = (bf16[512,256]{1,0:T(8,128)(2,1)S(1)}, bf16[512,256]{1,0:T(8,128)(2,1)}, u32[]{:S(2)}) copy-start(bf16[512,256]{1,0:T(8,128)(2,1)} %param.8) | copy-start | bytes 786436
  3.2 2.8 %copy-start.3 = (bf16[512,256]{1,0:T(8,128)(2,1)S(1)}, bf16[512,256]{1,0:T(8,128)(2,1)}, u32[]{:S(2)}) copy-start(bf16[512,256]{1,0:T(8,128)(2,1)} %param.9) | copy-start | bytes 786436
  5.0 44.9 %copy-start = (f32[512,128]{1,0:T(8,128)}, f32[512,128]{1,0:T(8,128)S(1)}, u32[]{:S(2)}) copy-start(f32[512,128]{1,0:T(8,128)S(1)} %get-tuple-element.16.cos_ref) | copy-start | bytes 786436
  5.0 44.9 %copy-start.1 = (f32[512,128]{1,0:T(8,128)}, f32[512,128]{1,0:T(8,128)S(1)}, u32[]{:S(2)}) copy-start(f32[512,128]{1,0:T(8,128)S(1)} %get-tuple-element.17.sin_ref) | copy-start | bytes 786436

commit v2 on v1

--- a/solution.py
+++ b/solution.py
@@ -12,6 +12,7 @@
 QUERY_BLOCK = 128
 TILE = 16
 SWAP_PARTS = 4
+GRANT = 24 << 20
 LANES = 128
 FAR = 1 << 28
 LOW = -1e30
@@ -341,13 +342,26 @@
 
 
 def attend_kernel(
-    shards, q_ref, cos_ref, sin_ref, cnt_ref, kv_ref, out_ref, q_s, top_s, sum_s, acc_s
+    shards,
+    chunks,
+    q_ref,
+    cos_ref,
+    sin_ref,
+    cnt_ref,
+    kv_ref,
+    out_ref,
+    q_s,
+    top_s,
+    sum_s,
+    acc_s,
+    table_s,
+    name_s,
 ):
     me = lax.axis_index("ctx")
     step = pl.program_id(0)
     blocks, groups, stack, _ = q_s.shape
     share = stack // QUERY_BLOCK
-    keys = kv_ref.shape[0]
+    keys = kv_ref.shape[0] // chunks
     shift = shards.bit_length() - 1
     factor = 1.4426950408889634 / HEAD_WIDTH**0.5
 
@@ -356,43 +370,35 @@
     own_start = jnp.sum(jnp.where(shard_row < me, counts, 0)[:, :1])
     own_count = jnp.sum(jnp.where(shard_row == me, counts, 0)[:, :1])
     live_blocks = (own_count + (QUERY_BLOCK - 1)) >> (QUERY_BLOCK.bit_length() - 1)
-
-    diagonal = shard_row == lax.broadcasted_iota(jnp.int32, counts.shape, 1)
-    count_row = jnp.sum(jnp.where(diagonal, counts, 0), axis=0, keepdims=True)
-    offset_row = jnp.sum(
-        jnp.where(shard_row < lax.broadcasted_iota(jnp.int32, counts.shape, 1), counts, 0),
-        axis=0,
-        keepdims=True,
-    )
     grid_shape = (keys, LANES)
     key_row = lax.broadcasted_iota(jnp.int32, grid_shape, 0)
-    source = lax.broadcasted_iota(jnp.int32, grid_shape, 1)
-    lead = ((key_row >> 4) - source) & (shards - 1)
-    taken = jnp.where(source < shards, (count_row + (shards - 1) - lead) >> shift, 0)
-    earlier = (
-        lax.broadcasted_iota(jnp.int32, (LANES, LANES), 0)
-        < lax.broadcasted_iota(jnp.int32, (LANES, LANES), 1)
-    )
-    start = jnp.dot(
-        taken.astype(jnp.float32).astype(jnp.bfloat16),
-        jnp.where(earlier, 1.0, 0.0).astype(jnp.bfloat16),
-        preferred_element_type=jnp.float32,
-    ).astype(jnp.int32)
-    within = step * TILE + (key_row & (TILE - 1)) - start
-    held = (within >= 0) & (within < taken)
-    names = jnp.min(
-        jnp.where(held, offset_row + within * shards + lead, FAR), axis=1, keepdims=True
-    )
-    first_name = jnp.min(names)
 
     @pl.when(step == 0)
     def _():
-        top_s[...] = jnp.full_like(top_s, LOW)
-        sum_s[...] = jnp.zeros_like(sum_s)
-        acc_s[...] = jnp.zeros_like(acc_s)
+        lane = lax.broadcasted_iota(jnp.int32, counts.shape, 1)
+        count_row = jnp.sum(jnp.where(shard_row == lane, counts, 0), axis=0, keepdims=True)
+        offset_row = jnp.sum(jnp.where(shard_row < lane, counts, 0), axis=0, keepdims=True)
+        source = lax.broadcasted_iota(jnp.int32, grid_shape, 1)
+        lead = ((key_row >> 4) - source) & (shards - 1)
+        taken = jnp.where(source < shards, (count_row + (shards - 1) - lead) >> shift, 0)
+        earlier = (
+            lax.broadcasted_iota(jnp.int32, (LANES, LANES), 0)
+            < lax.broadcasted_iota(jnp.int32, (LANES, LANES), 1)
+        )
+        start = jnp.dot(
+            taken.astype(jnp.float32).astype(jnp.bfloat16),
+            jnp.where(earlier, 1.0, 0.0).astype(jnp.bfloat16),
+            preferred_element_type=jnp.float32,
+        ).astype(jnp.int32)
+        table_s[0] = (key_row & (TILE - 1)) - start
+        table_s[1] = taken
+        table_s[2] = offset_row + lead
 
         @pl.loop(0, live_blocks)
         def _(b):
+            top_s[b] = jnp.full_like(top_s[b], LOW)
+            sum_s[b] = jnp.zeros_like(sum_s[b])
+            acc_s[b] = jnp.zeros_like(acc_s[b])
             at = pl.ds(pl.multiple_of(b * QUERY_BLOCK, QUERY_BLOCK), QUERY_BLOCK)
             cosine, sine = cos_ref[at, :], sin_ref[at, :]
             for g in range(groups):
@@ -402,34 +408,61 @@
                     turned = x * cosine + pltpu.roll(x, HEAD_WIDTH // 2, 1) * sine
                     q_s[b, g, pl.ds(h * QUERY_BLOCK, QUERY_BLOCK), :] = turned.astype(jnp.bfloat16)
 
+    firsts, last_name = [], None
+    for j in range(chunks):
+        within = table_s[0] + (step * chunks + j) * TILE
+        held = (within >= 0) & (within < table_s[1])
+        names = jnp.min(
+            jnp.where(held, table_s[2] + (within << shift), FAR), axis=1, keepdims=True
+        )
+        name_s[pl.ds(j * keys, keys), :] = names
+        firsts.append(jnp.min(names))
+        last = jnp.max(names)
+        last_name = last if last_name is None else jnp.maximum(last_name, last)
+
+    def update(b, first_query, used, masked):
+        rows = pl.ds(0, used * keys)
+        scores = []
+        for g in range(groups):
+            key = kv_ref[rows, pl.ds(g * HEAD_WIDTH, HEAD_WIDTH)]
+            scores.append(
+                lax.dot_general(
+                    key, q_s[b, g], (((1,), (1,)), ((), ())), preferred_element_type=jnp.float32
+                )
+            )
+        if masked:
+            query = first_query + lax.broadcasted_iota(
+                jnp.int32, (used * keys, QUERY_BLOCK), 1
+            )
+            bias = jnp.where(name_s[rows, :] <= query, 0.0, LOW)
+            bias = jnp.concatenate([bias] * share, axis=1)
+            scores = [x + bias for x in scores]
+        for g in range(groups):
+            value = kv_ref[rows, pl.ds((groups + g) * HEAD_WIDTH, HEAD_WIDTH)]
+            old = top_s[b, g]
+            top = jnp.maximum(old, jnp.max(scores[g], axis=0, keepdims=True))
+            terms = jnp.exp2((scores[g] - top) * factor)
+            rescale = jnp.exp2((old - top) * factor)
+            top_s[b, g] = top
+            sum_s[b, g] = sum_s[b, g] * rescale + jnp.sum(terms, axis=0, keepdims=True)
+            acc_s[b, g] = acc_s[b, g] * rescale + lax.dot_general(
+                value,
+                terms.astype(jnp.bfloat16),
+                (((0,), (0,)), ((), ())),
+                preferred_element_type=jnp.float32,
+            )
+
     @pl.loop(0, live_blocks)
     def _(b):
         first_query = own_start + b * QUERY_BLOCK
-
-        @pl.when(first_name < first_query + QUERY_BLOCK)
-        def _():
-            query = first_query + lax.broadcasted_iota(jnp.int32, (keys, QUERY_BLOCK), 1)
-            bias = jnp.where(names <= query, 0.0, LOW)
-            bias = jnp.concatenate([bias] * share, axis=1)
-            for g in range(groups):
-                key = kv_ref[:, pl.ds(g * HEAD_WIDTH, HEAD_WIDTH)]
-                value = kv_ref[:, pl.ds((groups + g) * HEAD_WIDTH, HEAD_WIDTH)]
-                scores = lax.dot_general(
-                    key, q_s[b, g], (((1,), (1,)), ((), ())), preferred_element_type=jnp.float32
-                )
-                scores = scores * factor + bias
-                old = top_s[b, g]
-                top = jnp.maximum(old, jnp.max(scores, axis=0, keepdims=True))
-                terms = jnp.exp2(scores - top)
-                rescale = jnp.exp2(old - top)
-                top_s[b, g] = top
-                sum_s[b, g] = sum_s[b, g] * rescale + jnp.sum(terms, axis=0, keepdims=True)
-                acc_s[b, g] = acc_s[b, g] * rescale + lax.dot_general(
-                    value,
-                    terms.astype(jnp.bfloat16),
-                    (((0,), (0,)), ((), ())),
-                    preferred_element_type=jnp.float32,
-                )
+        needed = sum((f < first_query + QUERY_BLOCK).astype(jnp.int32) for f in firsts)
+        plain = last_name <= first_query
+        for used in range(1, chunks + 1):
+            chosen = needed == used
+            if used == chunks:
+                pl.when(plain)(functools.partial(update, b, first_query, used, False))
+                chosen = chosen & jnp.logical_not(plain)
+            pl.when(chosen)(functools.partial(update, b, first_query, used, True))
 
     @pl.when(step == pl.num_programs(0) - 1)
     def _():
@@ -454,21 +487,23 @@
 def attend(q_home, cosine, sine, cnt_all, kv_all, shards):
     slots, features = q_home.shape
     pieces, keys, width = kv_all.shape
+    chunks = 3 if pieces % 3 == 0 and shards <= 32 else 1
+    kv_all = kv_all.reshape(pieces * keys, width)
     groups = width // (2 * HEAD_WIDTH)
     share = features // HEAD_WIDTH // groups
     blocks = slots // QUERY_BLOCK
     stack = share * QUERY_BLOCK
     whole = lambda a: pl.BlockSpec(a.shape, lambda i: (0,) * a.ndim)
     return pl.pallas_call(
-        functools.partial(attend_kernel, shards),
+        functools.partial(attend_kernel, shards, chunks),
         out_shape=jax.ShapeDtypeStruct((slots, features), jnp.bfloat16),
-        grid=(pieces,),
+        grid=(pieces // chunks,),
         in_specs=[
             whole(q_home),
             whole(cosine),
             whole(sine),
             whole(cnt_all),
-            pl.BlockSpec((None, keys, width), lambda i: (i, 0, 0)),
+            pl.BlockSpec((chunks * keys, width), lambda i: (i, 0)),
         ],
         out_specs=pl.BlockSpec((slots, features), lambda i: (0, 0)),
         scratch_shapes=[
@@ -476,7 +511,10 @@
             pltpu.VMEM((blocks, groups, 1, stack), jnp.float32),
             pltpu.VMEM((blocks, groups, 1, stack), jnp.float32),
             pltpu.VMEM((blocks, groups, HEAD_WIDTH, stack), jnp.float32),
+            pltpu.VMEM((3, keys, LANES), jnp.int32),
+            pltpu.VMEM((chunks * keys, 1), jnp.int32),
         ],
+        compiler_params=pltpu.CompilerParams(vmem_limit_bytes=GRANT),
         name="attend",
     )(q_home, cosine, sine, cnt_all, kv_all)
 
@@ -564,6 +602,7 @@
             ],
             out_specs=pl.BlockSpec((slots, tile), lambda i, h, c: (0, i)),
         ),
+        compiler_params=pltpu.CompilerParams(vmem_limit_bytes=GRANT),
         name="project",
     )(head, counts, mine, theirs, weight, swapped, gains)
 

time: 99.1 us -> 94.5 us (0.954)
  the two profiles are of different devices: /device:TPU:29 before, /device:TPU:31 now
where the time goes in v2:
time: 94.5 us; the launch traced here: 94.9 us
  Pallas kernels  76.2 us (81%)
  local copies, waits for them, and re-layouts  15.2 us (16%)
  other arithmetic  2.71 us (3%)
    pallas_call x1, Pallas kernels, spread(): pl.pallas_call(functools.partial(spread_kernel, shards), out_shape=(jax.S...  42.3 us
    pallas_call x1, Pallas kernels, attend(): pl.pallas_call(functools.partial(attend_kernel, shards, chunks), out_shap...  19.2 us
    unnamed x22, local copies, waits for them, and re-layouts  11.5 us
    pallas_call x1, Pallas kernels, project(): pl.pallas_call(project_kernel, out_shape=jax.ShapeDtypeStruct((slots, hal...  8.87 us
    pallas_call x1, Pallas kernels, trade(): pl.pallas_call(trade_kernel, out_shape=jax.ShapeDtypeStruct(mine.shape, m...  5.88 us

profile of v2, /device:TPU:31, one launch (start us, length us, event | category | flops | bytes accessed | tf_op | source)
XLA Modules:
  0.0 94.9 jit_solution(5420057679825822572)
XLA Ops:
  0.0 0.0 copy-start.9
  0.7 0.7 convert_element_type.9
  1.4 0.6 broadcast_in_dim.5.cnt_ref
  2.0 1.2 %reshape.28 = f32[512,2,128]{2,1,0:T(2,128)S(1)} reshape(bf16[512,256]{1,0:T(8,128)(2,1)} %param.8) | data formatting | bytes 786432 | tf_op jit(solution)/shard_map/reshape | solution.py:39
  3.2 0.0 copy-start.10
  3.2 0.6 fusion.2
  3.8 1.0 %fusion.1 = (f32[512,64]{1,0:T(8,128)S(1)}, f32[512,64]{1,0:T(8,128)S(1)}, f32[512,64]{1,0:T(8,128)S(1)}) fusion(f32[64]{0:T(128)S(1)} %negate_power_fusion, f32[512]{0:T(512)S(1)} %convert_element_type.9), kind=kLoop, calls=%fused_computation.10 | loop fusion | flops 65536 | bytes 395520 | tf_op jit(solution)/shard_map/neg | solution.py:33
  4.8 0.2 pad_maximum_fusion.1
  5.0 0.6 maximum_multiply_fusion
  5.7 0.2 mul.42
  5.9 0.0 copy-done.9
  5.9 0.1 fusion
  6.0 0.0 copy-done.10
  6.1 1.1 %copy.14 = bf16[32,16,512]{2,0,1:T(8,128)(2,1)} copy(bf16[32,16,512]{2,1,0:T(8,128)(2,1)S(1)} %bitcast.24) | data formatting | bytes 1048576 | tf_op jit(solution)/shard_map/reshape | solution.py:619
  7.2 0.0 copy-start.6
  7.2 42.3 %spread.1 = (bf16[9,16,16,512]{3,2,1,0:T(8,128)(2,1)}, s32[16,8,128]{2,1,0:T(8,128)}, bf16[1024,2048]{1,0:T(8,128)(2,1)}) custom-call(bf16[16,32,512]{2,1,0:T(8,128)(2,1)} %bitcast.22, s32[8,128]{1,0:T(8,128)} %broadcast_in_dim.5.cnt_ref, bf16[1024,4096]{1,0:T(8,128)(2,1)} %own_w.1), custom_call_target="tpu_custom_call" | custom-call | tf_op jit(solution)/shard_map/spread/pallas_call | solution.py:314
  49.4 0.0 copy-start.8
  49.5 0.0 copy-done.6
  49.5 0.0 copy-start.5
  49.5 1.7 %copy-done.5 = bf16[9,16,16,512]{3,2,1,0:T(8,128)(2,1)S(1)} copy-done((bf16[9,16,16,512]{3,2,1,0:T(8,128)(2,1)S(1)}, bf16[9,16,16,512]{3,2,1,0:T(8,128)(2,1)}, u32[]{:S(2)}) %copy-start.5) | copy-done | bytes 2359320
  51.1 0.0 copy-start.7
  51.1 0.8 copy-done.7
  52.0 19.2 %attend.1.mine_ref = bf16[512,1024]{1,0:T(8,128)(2,1)S(1)} custom-call(bf16[512,1024]{1,0:T(8,128)(2,1)S(1)} %copy-done.6, f32[512,128]{1,0:T(8,128)S(1)} %get-tuple-element.16.cos_ref, f32[512,128]{1,0:T(8,128)S(1)} %get-tuple-element.17.sin_ref, s32[16,8,128]{2,1,0:T(8,128)S(1)} %copy-done.7, bf16[2304,512]{1,0:T(8,128)(2,1)S(1)} %bitcast.19), custom_call_target="tpu_custom_call" | custom-call | tf_op jit(solution)/shard_map/attend/pallas_call | solution.py:497
  71.2 0.0 copy-start.1
  71.2 1.0 %copy-done.1 = bf16[512,1024]{1,0:T(8,128)(2,1)} copy-done((bf16[512,1024]{1,0:T(8,128)(2,1)}, bf16[512,1024]{1,0:T(8,128)(2,1)S(1)}, u32[]{:S(2)}) %copy-start.1) | copy-done | bytes 1048600
  72.2 5.9 %trade.1.theirs_ref = bf16[512,1024]{1,0:T(8,128)(2,1)} custom-call(bf16[512,1024]{1,0:T(8,128)(2,1)} %copy-done.1), custom_call_target="tpu_custom_call" | custom-call | tf_op jit(solution)/shard_map/trade/pallas_call | solution.py:547
  78.0 0.0 copy-done.8
  78.0 0.0 copy-start
  78.1 3.4 %copy-done = bf16[1024,4096]{1,0:T(8,128)(2,1)S(1)} copy-done((bf16[1024,4096]{1,0:T(8,128)(2,1)S(1)}, bf16[1024,4096]{1,0:T(8,128)(2,1)}, u32[]{:S(2)}) %copy-start) | copy-done | bytes 8388632
  81.4 0.0 copy-start.2
  81.4 1.2 %copy-done.2 = bf16[512,1024]{1,0:T(8,128)(2,1)S(1)} copy-done((bf16[512,1024]{1,0:T(8,128)(2,1)S(1)}, bf16[512,1024]{1,0:T(8,128)(2,1)}, u32[]{:S(2)}) %copy-start.2) | copy-done | bytes 1048600
  82.7 0.0 copy-start.3
  82.7 2.2 %copy-done.3 = bf16[1024,2048]{1,0:T(8,128)(2,1)S(1)} copy-done((bf16[1024,2048]{1,0:T(8,128)(2,1)S(1)}, bf16[1024,2048]{1,0:T(8,128)(2,1)}, u32[]{:S(2)}) %copy-start.3) | copy-done | bytes 4194328
  84.8 0.0 copy-start.4
  84.8 1.2 %copy-done.4 = bf16[512,1024]{1,0:T(8,128)(2,1)S(1)} copy-done((bf16[512,1024]{1,0:T(8,128)(2,1)S(1)}, bf16[512,1024]{1,0:T(8,128)(2,1)}, u32[]{:S(2)}) %copy-start.4) | copy-done | bytes 1048600
  86.1 8.9 %project.1 = bf16[512,2048]{1,0:T(8,128)(2,1)} custom-call(s32[1]{0:T(128)} %bitcast.head_ref, s32[1]{0:T(128)} %copy.15.count_ref, bf16[512,1024]{1,0:T(8,128)(2,1)S(1)} %copy-done.2, bf16[512,1024]{1,0:T(8,128)(2,1)S(1)} %copy-done.4, bf16[1024,4096]{1,0:T(8,128)(2,1)S(1)} %copy-done, bf16[1024,2048]{1,0:T(8,128)(2,1)S(1)} %copy-done.3, f32[4,128]{1,0:T(4,128)S(1)} %bitcast.20), custom_call_target="tpu_custom_call" | custom-call | tf_op jit(solution)/shard_map/project/pallas_call | solution.py:590
  (2 shorter events, 0.0 us)
Async XLA Ops:
  0.0 5.9 %copy-start.9 = (bf16[512,256]{1,0:T(8,128)(2,1)S(1)}, bf16[512,256]{1,0:T(8,128)(2,1)}, u32[]{:S(2)}) copy-start(bf16[512,256]{1,0:T(8,128)(2,1)} %param.8) | copy-start | bytes 786436
  3.2 2.8 %copy-start.10 = (bf16[512,256]{1,0:T(8,128)(2,1)S(1)}, bf16[512,256]{1,0:T(8,128)(2,1)}, u32[]{:S(2)}) copy-start(bf16[512,256]{1,0:T(8,128)(2,1)} %param.9) | copy-start | bytes 786436
  7.2 42.3 %copy-start.6 = (bf16[512,1024]{1,0:T(8,128)(2,1)S(1)}, bf16[512,1024]{1,0:T(8,128)(2,1)}, u32[]{:S(2)}) copy-start(bf16[512,1024]{1,0:T(8,128)(2,1)} %q_ref.1) | copy-start | bytes 3145732
  49.4 28.6 %copy-start.8 = (f32[512]{0:T(512)S(1)}, f32[512]{0:T(512)}, u32[]{:S(2)}) copy-start(f32[512]{0:T(512)} %param.11) | copy-start | bytes 6148
  49.5 1.7 %copy-start.5 = (bf16[9,16,16,512]{3,2,1,0:T(8,128)(2,1)S(1)}, bf16[9,16,16,512]{3,2,1,0:T(8,128)(2,1)}, u32[]{:S(2)}) copy-start(bf16[9,16,16,512]{3,2,1,0:T(8,128)(2,1)} %get-tuple-element.9) | copy-start | bytes 7077892
  51.1 0.8 copy-start.7
  71.2 1.0 %copy-start.1 = (bf16[512,1024]{1,0:T(8,128)(2,1)}, bf16[512,1024]{1,0:T(8,128)(2,1)S(1)}, u32[]{:S(2)}) copy-start(bf16[512,1024]{1,0:T(8,128)(2,1)S(1)} %attend.1.mine_ref) | copy-start | bytes 3145732
  78.0 3.4 %copy-start = (bf16[1024,4096]{1,0:T(8,128)(2,1)S(1)}, bf16[1024,4096]{1,0:T(8,128)(2,1)}, u32[]{:S(2)}) copy-start(bf16[1024,4096]{1,0:T(8,128)(2,1)} %own_w.1) | copy-start | bytes 25165828
  81.4 1.2 %copy-start.2 = (bf16[512,1024]{1,0:T(8,128)(2,1)S(1)}, bf16[512,1024]{1,0:T(8,128)(2,1)}, u32[]{:S(2)}) copy-start(bf16[512,1024]{1,0:T(8,128)(2,1)} %copy-done.1) | copy-start | bytes 3145732
  82.7 2.2 %copy-start.3 = (bf16[1024,2048]{1,0:T(8,128)(2,1)S(1)}, bf16[1024,2048]{1,0:T(8,128)(2,1)}, u32[]{:S(2)}) copy-start(bf16[1024,2048]{1,0:T(8,128)(2,1)} %get-tuple-element.10.got_w) | copy-start | bytes 12582916
  84.8 1.2 %copy-start.4 = (bf16[512,1024]{1,0:T(8,128)(2,1)S(1)}, bf16[512,1024]{1,0:T(8,128)(2,1)}, u32[]{:S(2)}) copy-start(bf16[512,1024]{1,0:T(8,128)(2,1)} %trade.1.theirs_ref) | copy-start | bytes 3145732
